TPU v7x, 32 devices: a whole 2x2x4 slice. The times are simulated.
32 devices in a mesh: sensor: 2 (over y), tm: 16 (over z, x, core).
Axes of the slice: x: 2, y: 2, z: 4, core: 2. Of those that a mesh axis runs over, the one named last changes fastest.
Arguments:
- recording: bfloat16 [256, 16384], P('sensor', 'tm'), may hold values from -6 to 6
- spatial_w: bfloat16 [512, 256], P(None, 'sensor'), may hold values from -0.375 to 0.375
- conv_w: bfloat16 [3, 3, 512, 512], P(None, None, 'sensor'), may hold values from -0.15625 to 0.15625
- conv_b: float32 [3, 512], P(None, 'sensor'), may hold values from -3 to 3
- dilations: int32 [3], replicated, may hold values from 1 to 16, as said below
- valid_frames: int32 [16], P('tm'), may hold values from 512 to 1024, as said below
- key_w: bfloat16 [512, 512], P('sensor'), may hold values from -0.25 to 0.25
- value_w: bfloat16 [512, 512], P('sensor'), may hold values from -0.25 to 0.25
- queries: bfloat16 [512, 2048], P('sensor'), may hold values from -60 to 60
Outputs:
- features: bfloat16 [512, 16384], P('sensor', 'tm')
- attended: bfloat16 [512, 2048], P('sensor')
Inputs may be any that keep to these rules, and one draw needn't show every extreme that they name: `dilations`: one layer has dilation exactly 16 and another exactly 1. `valid_frames`: one block is full and one holds exactly half of its 1024 frames.
All inputs are finite; a program needn't handle non-finite values.
Results may differ from a plain program's by a relative error of at most 0.015.
The roundings to bfloat16 on the way count: a program that leaves them out, or rounds other values in their place, can miss the bound.
Values may be sent and summed in bfloat16 or wider, within the bound.
No kernel may reach another device: no remote copies, remote signals or barrier semaphores. Data moves between devices by JAX's collectives and lax.ppermute only.
A program may use at most 64 MiB of HBM per device.

v0:
```python
import math
import jax
import jax.numpy as jnp
from jax import lax
from jax.sharding import PartitionSpec as P

HD = 64
LATENTS = 2048
LAYERS = 3
DMAX = 16


def padded(cells, sides, width):
    for axis, dim in sides:
        count = lax.axis_size(axis)
        ends = count - 1
        head = lax.slice_in_dim(cells, 0, width, axis=dim)
        tail = lax.slice_in_dim(cells, cells.shape[dim] - width, cells.shape[dim], axis=dim)
        cells = jnp.concatenate(
            [
                lax.ppermute(tail, axis, [(i, (i + 1) % count) for i in range(ends)]),
                cells,
                lax.ppermute(head, axis, [((i + 1) % count, i) for i in range(ends)]),
            ],
            axis=dim,
        )
    return cells


def tap_folder(kernels, dilation, frames, margin):

    def add_taps(running, portion, first_row):
        portion = jnp.pad(portion, ((0, 0), (margin, margin)))
        for tap_index in range(3):
            kernel = kernels[tap_index]
            offset = DMAX + (tap_index - 1) * dilation
            shifted = lax.dynamic_slice_in_dim(portion, offset, frames, 1)
            running = running + jnp.dot(kernel, shifted, preferred_element_type=jnp.float32)
        return running

    return add_taps


def on_device(
    recording, spatial_w, conv_w, conv_b, dilations, valid_frames, key_w, value_w, queries
):
    frames = recording.shape[1]
    ch_loc = conv_w.shape[2]
    hidden = lax.psum_scatter(
        jnp.dot(spatial_w, recording, preferred_element_type=jnp.float32),
        "sensor",
        scatter_dimension=0,
        tiled=True,
    ).astype(jnp.bfloat16)
    reach = 3 * DMAX
    extended = padded(hidden, (("tm", 1),), reach)
    span = frames + 2 * reach
    position = lax.axis_index("tm") * frames - reach + jnp.arange(span, dtype=jnp.int32)
    inside = (position >= 0) & (position < frames * lax.axis_size("tm"))
    for layer in range(LAYERS):
        initial = jnp.broadcast_to(conv_b[layer][:, None], (ch_loc, span))
        folder = tap_folder(conv_w[layer], dilations[layer], span, DMAX)
        preact = folder(
            initial, lax.all_gather(extended, "sensor", axis=0, tiled=True), jnp.int32(0)
        )
        updated = extended.astype(jnp.float32) + jax.nn.gelu(preact, approximate=False)
        extended = jnp.where(inside[None, :], updated, 0.0).astype(jnp.bfloat16)
    hidden = extended[:, reach : reach + frames]
    portion = lax.all_gather(hidden, "sensor", axis=0, tiled=True)
    key_rows = jnp.dot(key_w, portion, preferred_element_type=jnp.float32)
    value_rows = jnp.dot(value_w, portion, preferred_element_type=jnp.float32)
    head_count = key_w.shape[0] // HD
    key_heads = key_rows.astype(jnp.bfloat16).reshape(head_count, HD, frames)
    value_heads = value_rows.astype(jnp.bfloat16).reshape(head_count, HD, frames)
    frame_mask = jnp.arange(frames, dtype=jnp.int32) < valid_frames[0]
    block_rows = min(LATENTS, 512)
    block_count = LATENTS // block_rows
    query_blocks = queries.reshape(head_count, HD, block_count, block_rows).transpose(2, 0, 1, 3)
    scale = 1.0 / math.sqrt(HD)

    def attend(query_block):
        scores = (
            jnp.einsum("hdq,hdt->hqt", query_block, key_heads, preferred_element_type=jnp.float32)
            * scale
        )
        scores = jnp.where(frame_mask[None, None, :], scores, -jnp.inf)
        peaks = jnp.max(scores, axis=2)
        probs = jnp.where(frame_mask[None, None, :], jnp.exp(scores - peaks[:, :, None]), 0.0)
        totals = jnp.sum(probs, axis=2)
        weighted = jnp.einsum(
            "hqt,hdt->hdq",
            probs.astype(jnp.bfloat16),
            value_heads,
            preferred_element_type=jnp.float32,
        )
        return (peaks, totals, weighted)

    peaks, totals, weighted = lax.map(attend, query_blocks)
    peaks = peaks.transpose(1, 0, 2).reshape(head_count, LATENTS)
    totals = totals.transpose(1, 0, 2).reshape(head_count, LATENTS)
    weighted = weighted.transpose(1, 2, 0, 3).reshape(head_count, HD, LATENTS)
    global_peaks = lax.pmax(peaks, "tm")
    rescale = jnp.exp(peaks - global_peaks)
    totals, weighted = lax.psum((totals * rescale, weighted * rescale[:, None, :]), "tm")
    attended = (
        (weighted / totals[:, None, :]).reshape(head_count * HD, LATENTS).astype(jnp.bfloat16)
    )
    return (hidden, attended)


def solution(mesh):
    return jax.shard_map(
        on_device,
        mesh=mesh,
        in_specs=(
            P("sensor", "tm"),
            P(None, "sensor"),
            P(None, None, "sensor", None),
            P(None, "sensor"),
            P(),
            P("tm"),
            P("sensor", None),
            P("sensor", None),
            P("sensor", None),
        ),
        out_specs=(P("sensor", "tm"), P("sensor", None)),
        check_vma=False,
    )
```

profile of v0, /device:TPU:0, one launch (start us, length us, event | category | flops | bytes accessed | tf_op | source)
XLA Modules:
  0.0 366.2 jit_solution(9976685040315797149)
XLA Ops:
  8.1 2.7 fusion.128
  10.9 34.7 %reduce-scatter.2.cloned.1.call-done = f32[256,1024]{0,1:T(8,128)} async-done(((f32[512,1024]{0,1:T(8,128)}), f32[256,1024]{0,1:T(8,128)}) %reduce-scatter.2.cloned.1.call-update) | async-done | bytes 1048592 | tf_op jit(solution)/shard_map/reduce_scatter | solution.py:49
  45.6 1.4 convert_element_type.46
  47.1 1.6 collective-permute-start
  50.0 3.2 collective-permute-done.1
  56.7 22.1 %all-gather.5.cloned.1.call-done = bf16[512,1120]{0,1:T(8,128)(2,1)} async-done(((bf16[256,1120]{0,1:T(8,128)(2,1)}), bf16[512,1120]{0,1:T(8,128)(2,1)}) %all-gather.5.cloned.1.call-update) | async-done | bytes 1146896 | tf_op jit(solution)/shard_map/all_gather | solution.py:64
  78.8 1.9 fusion.72
  81.2 4.2 %fusion.26 = bf16[256,1120]{0,1:T(8,128)(2,1)} fusion(f32[1120,256]{1,0:T(8,128)S(1)} %fusion.72, f32[1120,256]{1,0:T(8,128)S(1)} %convolution_add_fusion.7, bf16[512,1120]{0,1:T(8,128)(2,1)S(1)} %copy-done.6, pred[1120]{0:T(1024)(128)(4,1)S(1)} %fusion.111, bf16[3,3,256,512]{3,2,1,0:T(8,128)(2,1)S(1)} %copy-done.9, ...), kind=kOutput, calls=%fused_computation.38 | convolution fusion | flops 315105280 | bytes 4851712 | tf_op jit(solution)/shard_map/dot_general | solution.py:38
  87.4 20.5 %all-gather.7.cloned.1.call-done = bf16[512,1120]{0,1:T(8,128)(2,1)} async-done(((bf16[256,1120]{0,1:T(8,128)(2,1)}), bf16[512,1120]{0,1:T(8,128)(2,1)}) %all-gather.7.cloned.1.call-update) | async-done | bytes 1146896 | tf_op jit(solution)/shard_map/all_gather | solution.py:64
  107.9 1.9 convolution_add_fusion.5
  110.9 4.0 %fusion.31 = bf16[256,1120]{0,1:T(8,128)(2,1)} fusion(bf16[256,1120]{0,1:T(8,128)(2,1)S(1)} %copy-done.8, f32[1120,256]{1,0:T(8,128)S(1)} %convolution_add_fusion.4, s32[]{:T(128)S(6)} %select_n.39, bf16[512,1120]{0,1:T(8,128)(2,1)S(1)} %copy-done.5, pred[1120]{0:T(1024)(128)(4,1)S(1)} %fusion.111, bf16[3,3,256,512]{3,2,1,0:T(8,128)(2,1)S(1)} %copy-done.9), kind=kOutput, calls=%fused_computation.43 | convolution fusion | flops 313384960 | bytes 3704836 | tf_op jit(solution)/shard_map/dot_general | solution.py:38
  116.7 20.7 %all-gather.9.cloned.1.call-done = bf16[512,1120]{0,1:T(8,128)(2,1)} async-done(((bf16[256,1120]{0,1:T(8,128)(2,1)}), bf16[512,1120]{0,1:T(8,128)(2,1)}) %all-gather.9.cloned.1.call-update) | async-done | bytes 1146896 | tf_op jit(solution)/shard_map/all_gather | solution.py:64
  137.5 1.9 convolution_add_fusion.2
  139.8 2.6 bitcast_abs_fusion
  146.2 20.1 %all-gather.11.cloned.1.call-done = bf16[512,1024]{0,1:T(8,128)(2,1)} async-done(((bf16[256,1024]{0,1:T(8,128)(2,1)}), bf16[512,1024]{0,1:T(8,128)(2,1)}) %all-gather.11.cloned.1.call-update) | async-done | bytes 1048592 | tf_op jit(solution)/shard_map/all_gather | solution.py:69
  166.3 1.8 convolution_convert_fusion.1
  168.6 28.8 %while.15 = (s32[]{:T(128)}, f32[4,4,512]{2,1,0:T(4,128)S(1)}, f32[4,4,512]{2,1,0:T(4,128)S(1)}, f32[4,4,64,512]{3,2,1,0:T(8,128)}, bf16[4,4,64,512]{3,2,1,0:T(8...) while((s32[]{:T(128)}, f32[4,4,512]{2,1,0:T(4,128)S(1)}, ...), condition=%wide.region_4.5_spmd.clone, body=%wide.region_1.4_spmd.clone.sunk | while | flops 564130816 | bytes 27071080 | solution.py:98
  169.3 1.4 fusion.149
  170.7 2.9 fusion.151
  173.6 2.3 fusion.150
  177.9 2.9 fusion.151
  180.8 2.3 fusion.150
  185.1 2.8 fusion.151
  188.0 2.3 fusion.150
  192.3 2.9 fusion.151
  195.2 2.3 fusion.150
  197.5 61.0 %pmax.7 = f32[4,2048]{1,0:T(4,128)S(1)} all-reduce(f32[4,2048]{1,0:T(4,128)S(1)} %bitcast.276), channel_id=1, replica_groups=mesh['sensor'=2,'tm'=16] {'tm'}, use_global_device_ids=true, to_apply=%region_5.6 | all-reduce | flops 8192 | bytes 65536 | tf_op jit(solution)/shard_map/pmax | solution.py:102
  258.5 1.8 copy.36
  260.3 1.5 broadcast_multiply_fusion
  263.9 58.3 %psum.15 = f32[4,2048]{1,0:T(4,128)S(1)} all-reduce(f32[4,2048]{1,0:T(4,128)S(1)} %get-tuple-element.102), channel_id=1, replica_groups=mesh['sensor'=2,'tm'=16] {'tm'}, use_global_device_ids=true, to_apply=%region_7.8 | all-reduce | flops 8192 | bytes 65536 | tf_op jit(solution)/shard_map/psum | solution.py:104
  322.2 34.4 %all-reduce.5.cloned.1.call-done = f32[4,64,2048]{2,1,0:T(8,128)} async-done(((f32[4,64,2048]{2,1,0:T(8,128)}), f32[4,64,2048]{2,1,0:T(8,128)}) %all-reduce.5.cloned.1.call-update) | async-done | bytes 2097168 | tf_op jit(solution)/shard_map/psum | solution.py:104
  356.6 2.7 divide_convert_fusion
  (73 shorter events, 19.1 us)
Async XLA Ops:
  7.2 1.0 copy-start
  7.2 38.5 %reduce-scatter.2.cloned.1.call-start = ((), (), s32[]{:S(2)}) async-start(), calls=%async_computation.1 | async-start | bytes 3145728 | tf_op jit(solution)/shard_map/reduce_scatter | solution.py:49
  10.9 67.9 %all-gather.5.cloned.1.call-start = ((), (), s32[]{:S(2)}) async-start(), calls=%async_computation.2 | async-start | bytes 1720320 | tf_op jit(solution)/shard_map/all_gather | solution.py:64
  45.6 33.1 %copy-start.9 = (bf16[3,3,256,512]{3,2,1,0:T(8,128)(2,1)S(1)}, bf16[3,3,256,512]{3,2,1,0:T(8,128)(2,1)}, u32[]{:S(2)}) copy-start(bf16[3,3,256,512]{3,2,1,0:T(8,128)(2,1)} %param.13) | copy-start | bytes 7077892
  47.1 7.1 %copy-start.12 = (s32[3]{0:T(128)S(1)}, s32[3]{0:T(128)}, u32[]{:S(2)}) copy-start(s32[3]{0:T(128)} %param.15) | copy-start | bytes 40
  47.1 9.6 %copy-start.13 = (f32[3,256]{1,0:T(4,128)S(1)}, f32[3,256]{1,0:T(4,128)}, u32[]{:S(2)}) copy-start(f32[3,256]{1,0:T(4,128)} %param.14) | copy-start | bytes 9220
  47.1 2.9 collective-permute-start
  48.7 4.5 %collective-permute-start.1 = (bf16[256,48]{0,1:T(8,128)(2,1)S(1)}, bf16[256,48]{0,1:T(8,128)(2,1)S(1)}, u32[]{:S(2)}, u32[]{:S(2)}) collective-permute-start(bf16[256,48]{0,1:T(8,128)(2,1)S(1)} %get-tuple-element.115), channel_id=1, source_target_pairs={{1,0},{2,1},{3,2},{4,3},{5,4},{6,5},{7,6},{8,7},{9,8},{10,9},{11,1... | collective-permute-start | bytes 73736 | tf_op jit(solution)/shard_map/ppermute | solution.py:23
  54.1 53.9 %all-gather.7.cloned.1.call-start = ((), (), s32[]{:S(2)}) async-start(), calls=%async_computation.3 | async-start | bytes 1720320 | tf_op jit(solution)/shard_map/all_gather | solution.py:64
  78.8 1.9 copy-start.6
  85.4 52.0 %all-gather.9.cloned.1.call-start = ((), (), s32[]{:S(2)}) async-start(), calls=%async_computation.4 | async-start | bytes 1720320 | tf_op jit(solution)/shard_map/all_gather | solution.py:64
  107.9 1.9 copy-start.5
  109.8 1.1 copy-start.8
  114.9 51.4 %all-gather.11.cloned.1.call-start = ((), (), s32[]{:S(2)}) async-start(), calls=%async_computation.5 | async-start | bytes 1572864 | tf_op jit(solution)/shard_map/all_gather | solution.py:69
  137.5 1.9 copy-start.4
  142.6 1.1 copy-start.3
  143.6 1.5 copy-start.7
  144.9 211.7 %all-reduce.5.cloned.1.call-start = ((), (), s32[]{:S(2)}) async-start(), calls=%async_computation.6 | async-start | bytes 4194304 | tf_op jit(solution)/shard_map/psum | solution.py:104
  146.0 20.3 %copy-start.10 = (bf16[256,512]{1,0:T(8,128)(2,1)S(1)}, bf16[256,512]{1,0:T(8,128)(2,1)}, u32[]{:S(2)}) copy-start(bf16[256,512]{1,0:T(8,128)(2,1)} %param.17) | copy-start | bytes 786436
  146.2 21.9 %copy-start.11 = (bf16[256,512]{1,0:T(8,128)(2,1)S(1)}, bf16[256,512]{1,0:T(8,128)(2,1)}, u32[]{:S(2)}) copy-start(bf16[256,512]{1,0:T(8,128)(2,1)} %param.18) | copy-start | bytes 786436
  166.3 1.8 copy-start.2
  261.9 1.0 copy-start.1
Sparse Core Ops, SparseCore 0:
  11.0 34.6 reduce-scatter.1
  54.2 24.5 all-gather.4
  85.6 22.3 all-gather.6
  115.1 22.3 all-gather.8
  145.0 21.2 all-gather.10
  262.0 94.5 all-reduce.4
where the time goes:
time: 367 us; the launch traced here: 366 us
  waiting for transfers between devices  156 us (43%)
  blocking collectives  119 us (32%)
  matrix products  40 us (11%)
  between operations  20 us (5%)
  other arithmetic  19.8 us (5%)
  local copies, waits for them, and re-layouts  7.85 us (2%)
    all_gather x3, waiting for transfers between devices, on_device(): lax.all_gather(extended, 'sensor', axis=0, tiled=True)  63.3 us
    pmax x1, blocking collectives, on_device(): global_peaks = lax.pmax(peaks, 'tm')  61 us
    psum x1, blocking collectives, on_device(): lax.psum((totals * rescale, weighted * rescale[:, None, :]), 'tm')  58.3 us
    reduce_scatter x1, waiting for transfers between devices, on_device(): lax.psum_scatter(jnp.dot(spatial_w, recording, preferred_element_type=jnp...  34.7 us
    psum x1, waiting for transfers between devices, on_device(): lax.psum((totals * rescale, weighted * rescale[:, None, :]), 'tm')  34.4 us
    all_gather x1, waiting for transfers between devices, on_device(): portion = lax.all_gather(hidden, 'sensor', axis=0, tiled=True)  20.1 us
    dot_general x9, matrix products, add_taps(): jnp.dot(kernel, shifted, preferred_element_type=jnp.float32)  18 us
    dot_general x4, matrix products, attend(): jnp.einsum('hqt,hdt->hdq', probs.astype(jnp.bfloat16), value_heads, prefe...  11.4 us
  transfers between devices with their start and end apart: 8, of which 7 were waited for; matrix products, arithmetic and copies ran while one was open for 1% of the time, Pallas kernels for 0%

commit v1 on v0

--- a/solution.py
+++ b/solution.py
@@ -8,6 +8,18 @@
 LATENTS = 2048
 LAYERS = 3
 DMAX = 16
+
+
+def doubled_up(x, axis, dim):
+    ways, here, step = (lax.axis_size(axis), lax.axis_index(axis), x.shape[dim])
+    line, have = (x, 1)
+    while have < ways:
+        line = jnp.concatenate(
+            [line, lax.ppermute(line, axis, [(d, (d - have) % ways) for d in range(ways)])],
+            axis=dim,
+        )
+        have = 2 * have
+    return jnp.roll(line, here * step, axis=dim)
 
 
 def padded(cells, sides, width):
@@ -60,9 +72,7 @@
     for layer in range(LAYERS):
         initial = jnp.broadcast_to(conv_b[layer][:, None], (ch_loc, span))
         folder = tap_folder(conv_w[layer], dilations[layer], span, DMAX)
-        preact = folder(
-            initial, lax.all_gather(extended, "sensor", axis=0, tiled=True), jnp.int32(0)
-        )
+        preact = folder(initial, doubled_up(extended, "sensor", 0), jnp.int32(0))
         updated = extended.astype(jnp.float32) + jax.nn.gelu(preact, approximate=False)
         extended = jnp.where(inside[None, :], updated, 0.0).astype(jnp.bfloat16)
     hidden = extended[:, reach : reach + frames]

time: 367 us -> 348 us (0.948)
  waiting for transfers between devices: 156 us -> 129 us
  other arithmetic: 19.8 us -> 23.8 us
    all_gather x3 -> x0, waiting for transfers between devices: 63.3 us -> none  [on_device(): lax.all_gather(extended, 'sensor', axis=0, tiled=True)]
    ppermute x0 -> x3, waiting for transfers between devices: none -> 36.7 us  [doubled_up(): lax.ppermute(line, axis, [(d, (d - have) % ways) for d in range(ways)])]
    concatenate x0 -> x3, other arithmetic: none -> 5 us  [doubled_up(): return jnp.roll(line, here * step, axis=dim)]
where the time goes in v1:
time: 348 us; the launch traced here: 347 us
  waiting for transfers between devices  129 us (37%)
  blocking collectives  119 us (34%)
  matrix products  43.4 us (12%)
  other arithmetic  23.8 us (7%)
  between operations  19.9 us (6%)
  local copies, waits for them, and re-layouts  6.73 us (2%)
  starting transfers between devices  4.8 us (1%)
    pmax x1, blocking collectives, on_device(): global_peaks = lax.pmax(peaks, 'tm')  61 us
    psum x1, blocking collectives, on_device(): lax.psum((totals * rescale, weighted * rescale[:, None, :]), 'tm')  58.4 us
    ppermute x3, waiting for transfers between devices, doubled_up(): lax.ppermute(line, axis, [(d, (d - have) % ways) for d in range(ways)])  36.7 us
    reduce_scatter x1, waiting for transfers between devices, on_device(): lax.psum_scatter(jnp.dot(spatial_w, recording, preferred_element_type=jnp...  34.7 us
    psum x1, waiting for transfers between devices, on_device(): lax.psum((totals * rescale, weighted * rescale[:, None, :]), 'tm')  34.2 us
    dot_general x9, matrix products, add_taps(): jnp.dot(kernel, shifted, preferred_element_type=jnp.float32)  21.3 us
    all_gather x1, waiting for transfers between devices, on_device(): portion = lax.all_gather(hidden, 'sensor', axis=0, tiled=True)  20.3 us
    dot_general x4, matrix products, attend(): jnp.einsum('hqt,hdt->hdq', probs.astype(jnp.bfloat16), value_heads, prefe...  11.4 us
  transfers between devices with their start and end apart: 8, of which 7 were waited for; matrix products, arithmetic and copies ran while one was open for 1% of the time, Pallas kernels for 0%

profile of v1, /device:TPU:0, one launch (start us, length us, event | category | flops | bytes accessed | tf_op | source)
XLA Modules:
  0.0 347.3 jit_solution(6038045827443462995)
XLA Ops:
  8.1 2.7 fusion.141
  10.9 34.7 %reduce-scatter.2.cloned.1.call-done = f32[256,1024]{0,1:T(8,128)} async-done(((f32[512,1024]{0,1:T(8,128)}), f32[256,1024]{0,1:T(8,128)}) %reduce-scatter.2.cloned.1.call-update) | async-done | bytes 1048592 | tf_op jit(solution)/shard_map/reduce_scatter | solution.py:61
  46.9 1.6 collective-permute-start
  49.8 3.2 collective-permute-done.1
  56.3 11.1 %collective-permute-done.2 = bf16[256,1120]{0,1:T(8,128)(2,1)S(1)} collective-permute-done((bf16[256,1120]{0,1:T(8,128)(2,1)S(1)}, bf16[256,1120]{0,1:T(8,128)(2,1)S(1)}, u32[]{:S(2)}, u32[]{:S(2)}) %collective-permute-start.2) | collective-permute-done | bytes 573472 | tf_op jit(solution)/shard_map/ppermute | solution.py:18
  67.4 3.5 %fusion.40 = bf16[512,1120]{0,1:T(8,128)(2,1)S(1)} fusion(s32[]{:T(128)S(6)} %select_n.61, bf16[256,48]{0,1:T(8,128)(2,1)S(1)} %collective-permute-done, bf16[256,1024]{0,1:T(8,128)(2,1)S(1)} %convert_element_type.46, bf16[256,48]{0,1:T(8,128)(2,1)S(1)} %collective-permute-done.1, bf16[256,1120]{0,1:T(8,128)(2,1)S(1)} %collective-permute-done.2), kind=kLoop, calls=%fused_computation.69 | loop fusion | flops 9175040 | bytes 2293764 | tf_op jit(solution)/shard_map/jit(_roll_dynamic)/concatenate | solution.py:22
  70.9 1.5 convolution_add_fusion.8
  72.4 1.5 convolution_add_fusion.7
  73.9 4.7 %fusion.25 = bf16[256,1120]{0,1:T(8,128)(2,1)S(1)} fusion(f32[1120,256]{1,0:T(8,128)S(1)} %convolution_add_fusion.7, s32[]{:T(128)S(6)} %select_n.46, bf16[512,1120]{0,1:T(8,128)(2,1)S(1)} %fusion.40, pred[1120]{0:T(1024)(128)(4,1)S(1)} %fusion.124, bf16[3,3,256,512]{3,2,1,0:T(8,128)(2,1)} %param.15, bf16[256,48]{0,1:T(8,128)(2,1)S(1)} %collective-permute-done.1, ...), kind=kOutput, calls=%fused_computation.54 | convolution fusion | flops 314818560 | bytes 3703908 | tf_op jit(solution)/shard_map/dot_general | solution.py:50
  81.1 12.9 %collective-permute-done.3 = bf16[256,1120]{0,1:T(8,128)(2,1)S(1)} collective-permute-done((bf16[256,1120]{0,1:T(8,128)(2,1)S(1)}, bf16[256,1120]{0,1:T(8,128)(2,1)S(1)}, u32[]{:S(2)}, u32[]{:S(2)}) %collective-permute-start.3) | collective-permute-done | bytes 573472 | tf_op jit(solution)/shard_map/ppermute | solution.py:18
  94.8 1.5 convolution_add_fusion.5
  97.7 4.3 %fusion.30 = bf16[256,1120]{0,1:T(8,128)(2,1)S(1)} fusion(bf16[256,1120]{0,1:T(8,128)(2,1)S(1)} %fusion.25, f32[1120,256]{1,0:T(8,128)S(1)} %convolution_add_fusion.4, s32[]{:T(128)S(6)} %select_n.49, bf16[512,1120]{0,1:T(8,128)(2,1)S(1)} %fusion.35, pred[1120]{0:T(1024)(128)(4,1)S(1)} %fusion.124, bf16[3,3,256,512]{3,2,1,0:T(8,128)(2,1)} %param.15), kind=kOutput, calls=%fused_computation.59 | convolution fusion | flops 313384960 | bytes 3703908 | tf_op jit(solution)/shard_map/dot_general | solution.py:50
  104.6 12.6 %collective-permute-done.4 = bf16[256,1120]{0,1:T(8,128)(2,1)S(1)} collective-permute-done((bf16[256,1120]{0,1:T(8,128)(2,1)S(1)}, bf16[256,1120]{0,1:T(8,128)(2,1)S(1)}, u32[]{:S(2)}, u32[]{:S(2)}) %collective-permute-start.4) | collective-permute-done | bytes 573472 | tf_op jit(solution)/shard_map/ppermute | solution.py:18
  118.0 1.5 convolution_add_fusion.2
  120.9 3.6 %bitcast_abs_fusion = (f32[256,1120]{0,1:T(8,128)S(1)}, f32[256,1120]{0,1:T(8,128)S(1)}, f32[256,1120]{0,1:T(8,128)S(1)}, f32[256,1120]{0,1:T(8,128)S(1)}, f32[1120,256]{1,0:T(8,128)S(1)}) fusion(f32[1120,256]{1,0:T(8,128)S(1)} %convolution_add_fusion.1, bf16[3,3,256,512]{3,2,1,0:T(8,128)(2,1)} %param.15, s32[]{:T(128)S(6)} %select_n.52, ...), kind=kOutput, calls=%fused_computation.76 | convolution fusion | flops 310231040 | bytes 8290308 | tf_op jit(solution)/shard_map/dot_general | solution.py:50
  127.4 20.3 %all-gather.2.cloned.1.call-done = bf16[512,1024]{0,1:T(8,128)(2,1)} async-done(((bf16[256,1024]{0,1:T(8,128)(2,1)}), bf16[512,1024]{0,1:T(8,128)(2,1)}) %all-gather.2.cloned.1.call-update) | async-done | bytes 1048592 | tf_op jit(solution)/shard_map/all_gather | solution.py:79
  147.8 1.8 convolution_convert_fusion.1
  150.1 28.9 %while.15 = (s32[]{:T(128)}, f32[4,4,512]{2,1,0:T(4,128)S(1)}, f32[4,4,512]{2,1,0:T(4,128)S(1)}, f32[4,4,64,512]{3,2,1,0:T(8,128)}, bf16[4,4,64,512]{3,2,1,0:T(8...) while((s32[]{:T(128)}, f32[4,4,512]{2,1,0:T(4,128)S(1)}, ...), condition=%wide.region_4.6_spmd.clone, body=%wide.region_1.5_spmd.clone.sunk | while | flops 564130816 | bytes 27071080 | solution.py:108
  152.2 2.9 fusion.164
  155.0 2.3 fusion.163
  159.4 2.9 fusion.164
  162.2 2.3 fusion.163
  166.6 2.8 fusion.164
  169.4 2.3 fusion.163
  173.8 2.9 fusion.164
  176.7 2.3 fusion.163
  179.0 61.0 %pmax.7 = f32[4,2048]{1,0:T(4,128)S(1)} all-reduce(f32[4,2048]{1,0:T(4,128)S(1)} %bitcast.276), channel_id=1, replica_groups=mesh['sensor'=2,'tm'=16] {'tm'}, use_global_device_ids=true, to_apply=%region_5.7 | all-reduce | flops 8192 | bytes 65536 | tf_op jit(solution)/shard_map/pmax | solution.py:112
  240.0 1.8 copy.53
  241.8 1.5 broadcast_multiply_fusion
  245.4 58.4 %psum.15 = f32[4,2048]{1,0:T(4,128)S(1)} all-reduce(f32[4,2048]{1,0:T(4,128)S(1)} %get-tuple-element.111), channel_id=1, replica_groups=mesh['sensor'=2,'tm'=16] {'tm'}, use_global_device_ids=true, to_apply=%region_7.9 | all-reduce | flops 8192 | bytes 65536 | tf_op jit(solution)/shard_map/psum | solution.py:114
  303.8 34.2 %all-reduce.5.cloned.1.call-done = f32[4,64,2048]{2,1,0:T(8,128)} async-done(((f32[4,64,2048]{2,1,0:T(8,128)}), f32[4,64,2048]{2,1,0:T(8,128)}) %all-reduce.5.cloned.1.call-update) | async-done | bytes 2097168 | tf_op jit(solution)/shard_map/psum | solution.py:114
  338.1 2.7 divide_convert_fusion
  (61 shorter events, 24.2 us)
Async XLA Ops:
  7.2 1.0 copy-start
  7.2 38.5 %reduce-scatter.2.cloned.1.call-start = ((), (), s32[]{:S(2)}) async-start(), calls=%async_computation.1 | async-start | bytes 3145728 | tf_op jit(solution)/shard_map/reduce_scatter | solution.py:61
  10.9 42.8 %copy-start.6 = (s32[3]{0:T(128)S(1)}, s32[3]{0:T(128)}, u32[]{:S(2)}) copy-start(s32[3]{0:T(128)} %param.17) | copy-start | bytes 40
  10.9 45.4 %copy-start.7 = (f32[3,256]{1,0:T(4,128)S(1)}, f32[3,256]{1,0:T(4,128)}, u32[]{:S(2)}) copy-start(f32[3,256]{1,0:T(4,128)} %param.16) | copy-start | bytes 9220
  10.9 136.9 %all-gather.2.cloned.1.call-start = ((), (), s32[]{:S(2)}) async-start(), calls=%async_computation.2 | async-start | bytes 1572864 | tf_op jit(solution)/shard_map/all_gather | solution.py:79
  46.9 2.9 collective-permute-start
  48.5 4.5 %collective-permute-start.1 = (bf16[256,48]{0,1:T(8,128)(2,1)S(1)}, bf16[256,48]{0,1:T(8,128)(2,1)S(1)}, u32[]{:S(2)}, u32[]{:S(2)}) collective-permute-start(bf16[256,48]{0,1:T(8,128)(2,1)S(1)} %get-tuple-element.123), channel_id=1, source_target_pairs={{1,0},{2,1},{3,2},{4,3},{5,4},{6,5},{7,6},{8,7},{9,8},{10,9},{11,1... | collective-permute-start | bytes 73736 | tf_op jit(solution)/shard_map/ppermute | solution.py:35
  53.1 14.3 %collective-permute-start.2 = (bf16[256,1120]{0,1:T(8,128)(2,1)S(1)}, bf16[256,1120]{0,1:T(8,128)(2,1)S(1)}, u32[]{:S(2)}, u32[]{:S(2)}) collective-permute-start(bf16[256,1120]{0,1:T(8,128)(2,1)S(1)} %pad_maximum_fusion), channel_id=1, source_target_pairs={{0,16},{16,0},{1,17},{17,1},{2,18},{18,2},{3,19},{19,3},{4,20},{20... | collective-permute-start | bytes 1720328 | tf_op jit(solution)/shard_map/ppermute | solution.py:18
  78.5 15.5 %collective-permute-start.3 = (bf16[256,1120]{0,1:T(8,128)(2,1)S(1)}, bf16[256,1120]{0,1:T(8,128)(2,1)S(1)}, u32[]{:S(2)}, u32[]{:S(2)}) collective-permute-start(bf16[256,1120]{0,1:T(8,128)(2,1)S(1)} %fusion.25), channel_id=1, source_target_pairs={{0,16},{16,0},{1,17},{17,1},{2,18},{18,2},{3,19},{19,3},{4,20},{20... | collective-permute-start | bytes 1720328 | tf_op jit(solution)/shard_map/ppermute | solution.py:18
  102.0 15.2 %collective-permute-start.4 = (bf16[256,1120]{0,1:T(8,128)(2,1)S(1)}, bf16[256,1120]{0,1:T(8,128)(2,1)S(1)}, u32[]{:S(2)}, u32[]{:S(2)}) collective-permute-start(bf16[256,1120]{0,1:T(8,128)(2,1)S(1)} %fusion.30), channel_id=1, source_target_pairs={{0,16},{16,0},{1,17},{17,1},{2,18},{18,2},{3,19},{19,3},{4,20},{20... | collective-permute-start | bytes 1720328 | tf_op jit(solution)/shard_map/ppermute | solution.py:18
  124.8 1.4 copy-start.3
  126.1 212.0 %all-reduce.5.cloned.1.call-start = ((), (), s32[]{:S(2)}) async-start(), calls=%async_computation.3 | async-start | bytes 4194304 | tf_op jit(solution)/shard_map/psum | solution.py:114
  127.2 20.6 %copy-start.4 = (bf16[256,512]{1,0:T(8,128)(2,1)S(1)}, bf16[256,512]{1,0:T(8,128)(2,1)}, u32[]{:S(2)}) copy-start(bf16[256,512]{1,0:T(8,128)(2,1)} %param.19) | copy-start | bytes 786436
  127.4 22.1 %copy-start.5 = (bf16[256,512]{1,0:T(8,128)(2,1)S(1)}, bf16[256,512]{1,0:T(8,128)(2,1)}, u32[]{:S(2)}) copy-start(bf16[256,512]{1,0:T(8,128)(2,1)} %param.20) | copy-start | bytes 786436
  147.8 1.8 copy-start.2
  243.4 1.0 copy-start.1
Sparse Core Ops, SparseCore 0:
  11.0 34.6 reduce-scatter.1
  126.2 21.5 all-gather.1
  243.5 94.4 all-reduce.4
